TPU v7x, 32 devices: a whole 2x2x4 slice. The times are simulated.
32 devices in a mesh: dp: 8 (over z, x), tensor: 4 (over y, core).
Axes of the slice: x: 2, y: 2, z: 4, core: 2. Of those that a mesh axis runs over, the one named last changes fastest.
Arguments:
- tokens: bfloat16 [8192, 1024], P('dp'), may hold values from -17 to 17
- views: int32 [1], replicated, may hold values from 2 to 8, as said below
- ln1_gain: float32 [1024], replicated, may hold values from 0.5 to 1.5
- ln1_bias: float32 [1024], replicated, may hold values from -3 to 3
- w_query: bfloat16 [1024, 1024], P(None, 'tensor'), may hold values from -0.25 to 0.25
- w_key: bfloat16 [1024, 1024], P(None, 'tensor'), may hold values from -0.25 to 0.25
- w_value: bfloat16 [1024, 1024], P(None, 'tensor'), may hold values from -0.1875 to 0.1875
- w_out: bfloat16 [1024, 1024], P('tensor'), may hold values from -1.5 to 1.5
- ln2_gain: float32 [1024], replicated, may hold values from 0.5 to 1.5
- ln2_bias: float32 [1024], replicated, may hold values from -3 to 3
- w_up: bfloat16 [1024, 4096], P(None, 'tensor'), may hold values from -0.1875 to 0.1875
- w_down: bfloat16 [4096, 1024], P('tensor'), may hold values from -0.09375 to 0.09375
- cotangent: bfloat16 [8192, 1024], P('dp'), may hold values from -6 to 6
Outputs:
- mixed: bfloat16 [8192, 1024], P('dp')
- tokens_grad: bfloat16 [8192, 1024], P('dp')
- ln1_gain_grad: float32 [1024], replicated
- ln1_bias_grad: float32 [1024], replicated
- w_query_grad: float32 [1024, 1024], P(None, 'tensor')
- w_key_grad: float32 [1024, 1024], P(None, 'tensor')
- w_value_grad: float32 [1024, 1024], P(None, 'tensor')
- w_out_grad: float32 [1024, 1024], P('tensor')
- ln2_gain_grad: float32 [1024], replicated
- ln2_bias_grad: float32 [1024], replicated
- w_up_grad: float32 [1024, 4096], P(None, 'tensor')
- w_down_grad: float32 [4096, 1024], P('tensor')
Inputs may be any that keep to these rules, and one draw needn't show every extreme that they name: Exactly one scene has 8 views.
All inputs are finite; a program needn't handle non-finite values.
Results may differ from a plain program's by a relative error of at most 0.025.
Values may be sent and summed in bfloat16 or wider, within the bound.
A program may use at most 192 MiB of HBM per device.

v0:
```python
from functools import partial
import math

import jax
import jax.numpy as jnp
from jax import lax
from jax.experimental import pallas as pl
from jax.experimental.pallas import tpu as pltpu
from jax.sharding import PartitionSpec as P

HEAD_DIM = 64
VIEW_TOK = 1024
MAX_VIEWS = 8
LOG2E = math.log2(math.e)
VMEM_BYTES = 48 << 20
LOT = 128 << 10

norm_eps = 1e-05

bf16 = jnp.bfloat16
f32 = jnp.float32
dot = partial(jnp.dot, preferred_element_type=f32)


def contract(left, right, left_dim, right_dim):
    return lax.dot_general(
        left, right, (((left_dim,), (right_dim,)), ((), ())), preferred_element_type=f32
    )


def layer_norm(values, gain, shift):
    row_mean = jnp.mean(values, axis=-1, keepdims=True)
    centered = values - row_mean
    inverse = lax.rsqrt(jnp.mean(centered * centered, axis=-1, keepdims=True) + norm_eps)
    normed = centered * inverse
    return (normed * gain + shift, normed, inverse)


def norm_back(grad_norm, normed, inverse, gain):
    scaled = grad_norm * gain
    grad_input = inverse * (
        scaled
        - jnp.mean(scaled, axis=-1, keepdims=True)
        - normed * jnp.mean(scaled * normed, axis=-1, keepdims=True)
    )
    return (grad_input, jnp.sum(grad_norm * normed, axis=0), jnp.sum(grad_norm, axis=0))


def first_norm(core, tokens, gain, shift):
    row_count, width = tokens.shape
    block = row_count // 4

    def kernel(core_ref, tokens_ref, gain_ref, shift_ref, out_ref, normed_ref, inverse_ref):
        values, normed, inverse = layer_norm(
            tokens_ref[...].astype(f32), gain_ref[...], shift_ref[...]
        )
        out_ref[...] = values.astype(bf16)
        normed_ref[...] = normed
        inverse_ref[...] = inverse

    by_rows = pl.BlockSpec((block, width), lambda i, core_ref: (i, 0))
    row = pl.BlockSpec((1, width), lambda i, core_ref: (0, 0))
    return pl.pallas_call(
        kernel,
        grid_spec=pltpu.PrefetchScalarGridSpec(
            num_scalar_prefetch=1,
            grid=(4,),
            in_specs=[
                pl.BlockSpec((block, width), lambda i, core_ref: ((i + 2 * core_ref[0]) % 4, 0)),
                row,
                row,
            ],
            out_specs=[by_rows, by_rows, pl.BlockSpec((block, 1), lambda i, core_ref: (i, 0))],
        ),
        out_shape=[
            jax.ShapeDtypeStruct((row_count, width), bf16),
            jax.ShapeDtypeStruct((row_count, width), f32),
            jax.ShapeDtypeStruct((row_count, 1), f32),
        ],
        cost_estimate=pl.CostEstimate(
            flops=10 * row_count * width, bytes_accessed=8 * row_count * width, transcendentals=0
        ),
    )(core.reshape(1).astype(jnp.int32), tokens, gain.reshape(1, width), shift.reshape(1, width))


def sweep_forward(live_views, q_cols, kv, carry, last):
    count = q_cols.shape[1]
    keys = kv.shape[0]
    sum_rows = HEAD_DIM + 16
    bq, bk = 2048, 512

    def kernel(*refs):
        live_ref, q_ref, kv_ref = refs[:3]
        columns_ref = refs[-1]
        refs = refs[3:-1]
        if carry is not None:
            start = (refs[0][...], refs[1][...])
            refs = refs[2:]
        else:
            start = (jnp.full((1, bq), -1e30, f32), jnp.zeros((sum_rows, bq), f32))
        queries = jnp.concatenate([q_ref[...], jnp.zeros((HEAD_DIM, bq), bf16)], axis=0)

        @pl.when(pl.program_id(0) == 0)
        def _():
            columns_ref[HEAD_DIM:, :] = jnp.ones((16, keys), bf16)
            columns_ref[:HEAD_DIM, :] = kv_ref[...].T[HEAD_DIM:]

        def view_step(view, running):
            top, accum = running
            for part in range(VIEW_TOK // bk):
                first = pl.multiple_of(view * VIEW_TOK + part * bk, bk)
                scores = dot(kv_ref[pl.ds(first, bk), :], queries)
                new_top = jnp.maximum(top, jnp.max(scores, axis=0, keepdims=True))
                weights = jnp.exp2(scores - new_top).astype(bf16)
                accum = accum * jnp.exp2(top - new_top) + dot(
                    columns_ref[:, pl.ds(first, bk)], weights
                )
                top = new_top
            return (top, accum)

        top, accum = lax.fori_loop(0, live_ref[0], view_step, start)
        if last:
            total = accum[HEAD_DIM : HEAD_DIM + 1]
            heads_out = accum[:HEAD_DIM] / total
            refs[0][...] = heads_out
            refs[1][...] = heads_out.astype(bf16)
            refs[2][...] = top + jnp.log2(total)
        else:
            refs[0][...] = top
            refs[1][...] = accum

    def columns(rows):
        return pl.BlockSpec((rows, bq), lambda i: (0, i))

    in_specs = [
        pl.BlockSpec(memory_space=pltpu.SMEM),
        columns(HEAD_DIM),
        pl.BlockSpec(kv.shape, lambda i: (0, 0)),
    ]
    operands = [live_views, q_cols, kv]
    if carry is not None:
        in_specs += [columns(1), columns(sum_rows)]
        operands += list(carry)
    if last:
        shapes = [((HEAD_DIM, count), f32), ((HEAD_DIM, count), bf16), ((1, count), f32)]
    else:
        shapes = [((1, count), f32), ((sum_rows, count), f32)]
    return pl.pallas_call(
        kernel,
        grid=(count // bq,),
        in_specs=in_specs,
        out_specs=[columns(shape[0]) for shape, _ in shapes],
        out_shape=[jax.ShapeDtypeStruct(shape, kind) for shape, kind in shapes],
        scratch_shapes=[pltpu.VMEM((sum_rows, keys), bf16)],
        compiler_params=pltpu.CompilerParams(vmem_limit_bytes=VMEM_BYTES),
        cost_estimate=pl.CostEstimate(
            flops=16 * HEAD_DIM * count * keys, bytes_accessed=8 << 20, transcendentals=count * keys
        ),
    )(*operands)


MESH = pl.DeviceIdType.MESH


def greet(peers):
    barrier = pltpu.get_barrier_semaphore()
    for peer in peers:
        pl.semaphore_signal(barrier, inc=1, device_id=peer, device_id_type=MESH)
    pl.semaphore_wait(barrier, len(peers))


def window(start, size, axis):
    span = pl.ds(pl.multiple_of(start, size), size)
    return (span, slice(None)) if axis == 0 else (slice(None), span)


def exchange(number, ways, *items):
    def kernel(*refs):
        count = len(items)
        sources, targets = refs[:count], refs[count : 2 * count]
        own_sems, send_sems, recv_sems = refs[2 * count :]
        position = lax.axis_index("dp")
        place = position % (2 * ways) // 2
        base = position - 2 * place
        places = [lax.rem(place + distance, ways) for distance in range(ways)]
        greet([{"dp": base + 2 * places[distance]} for distance in range(1, ways)])
        copies = []
        for distance in range(1, ways):
            for index, (array, split, concat) in enumerate(items):
                size = array.shape[split] // ways
                copy = pltpu.make_async_remote_copy(
                    src_ref=sources[index].at[window(places[distance] * size, size, split)],
                    dst_ref=targets[index].at[
                        window(place * array.shape[concat], array.shape[concat], concat)
                    ],
                    send_sem=send_sems.at[index, distance],
                    recv_sem=recv_sems.at[index, distance],
                    device_id={"dp": base + 2 * places[distance]},
                    device_id_type=MESH,
                )
                copy.start()
                copies.append(copy)
        for index, (array, split, concat) in enumerate(items):
            size = array.shape[split] // ways
            copy = pltpu.make_async_copy(
                sources[index].at[window(place * size, size, split)],
                targets[index].at[
                    window(place * array.shape[concat], array.shape[concat], concat)
                ],
                own_sems.at[index],
            )
            copy.start()
            copies.append(copy)
        for copy in copies:
            copy.wait()

    def shape(array, split, concat):
        sizes = list(array.shape)
        sizes[split] //= ways
        sizes[concat] *= ways
        return jax.ShapeDtypeStruct(tuple(sizes), array.dtype)

    count = len(items)
    vmem = pl.BlockSpec(memory_space=pltpu.VMEM)
    moved = sum(array.size * array.dtype.itemsize for array, _, _ in items)
    return pl.pallas_call(
        kernel,
        in_specs=[vmem] * count,
        out_specs=[vmem] * count,
        out_shape=[shape(*item) for item in items],
        scratch_shapes=[
            pltpu.SemaphoreType.DMA((count,)),
            pltpu.SemaphoreType.DMA((count, ways)),
            pltpu.SemaphoreType.DMA((count, ways)),
        ],
        compiler_params=pltpu.CompilerParams(
            collective_id=number, has_side_effects=True, vmem_limit_bytes=16 << 20
        ),
        cost_estimate=pl.CostEstimate(flops=0, bytes_accessed=40 * moved, transcendentals=0),
    )(*[array for array, _, _ in items])


def sweep_backward(number, ways, bias, q_cols, g_cols, heads_out, kv_far, kv_own, log_norm, grads):
    count = q_cols.shape[1]
    keys = kv_own.shape[0]
    bq, bk = 1024, 512
    steps = 2 * keys // VIEW_TOK
    rows_of, width = grads[0].shape
    lot_rows = rows_of // steps
    half, part = lot_rows // 2, lot_rows // 2 // ways

    def kernel(*refs):
        masked = bias is not None
        bias_ref = refs[0] if masked else None
        refs = refs[1:] if masked else refs
        q_ref, g_ref, heads_ref, far_ref, own_ref, norm_ref = refs[:6]
        sources, pairs_ref, out_ref, results = refs[6:8], refs[8], refs[9], refs[10:12]
        total_ref, rows_ref, delta_ref, kv_ref, given_ref, met_ref, x_in, x_sums, z_in = refs[12:21]
        sems = refs[21:]
        position = lax.axis_index("dp")
        place = position % (2 * ways) // 2
        side = position % 2
        base = position - 2 * place
        across = {"dp": position + 1 - 2 * side}
        places = [lax.rem(place + distance, ways) for distance in range(ways)]
        peers = [{"dp": base + 2 * at} for at in places]
        greet([across] + peers[1:])

        def remote(source, target, kind, at, to):
            return pltpu.make_async_remote_copy(
                src_ref=source,
                dst_ref=target,
                send_sem=sems[2 * kind].at[at],
                recv_sem=sems[2 * kind + 1].at[at],
                device_id=to,
                device_id_type=MESH,
            )

        def over_x(which, lot):
            given = window(lot * lot_rows + (1 - side) * half, half, 0)
            slot = which * steps + lot
            return remote(sources[which].at[given], x_in.at[slot], 0, slot, across)

        def to_places(which, lot, distance):
            slot = which * steps + lot
            return remote(
                x_sums.at[slot, window(places[distance] * part, part, 0)[0]],
                z_in.at[slot, distance - 1],
                1,
                slot * ways + distance,
                peers[distance],
            )

        def from_place(which, lot, distance):
            slot = which * steps + lot
            mine = results[which].at[window(lot * lot_rows + side * half + place * part, part, 0)]
            return remote(mine, mine, 2, slot * ways + distance, peers[distance])

        def back_over_x(which, lot):
            mine = results[which].at[window(lot * lot_rows + side * half, half, 0)]
            return remote(mine, mine, 3, which * steps + lot, across)

        def far_pairs(view):
            span = window(view * VIEW_TOK, VIEW_TOK, 0)
            return remote(given_ref.at[span], met_ref.at[span], 4, view, across)

        def start_lot(lot):
            for which in range(2):
                over_x(which, lot).start()

        def reduce_across(lot):
            for which in range(2):
                slot = which * steps + lot
                over_x(which, lot).wait_recv()
                kept = sources[which][window(lot * lot_rows + side * half, half, 0)]
                x_sums[slot] = (kept.astype(f32) + x_in[slot].astype(f32)).astype(bf16)
                for distance in range(1, ways):
                    to_places(which, lot, distance).start()

        def reduce_places(lot):
            for which in range(2):
                slot = which * steps + lot
                total = x_sums[slot, window(place * part, part, 0)[0], :].astype(f32)
                for distance in range(1, ways):
                    to_places(which, lot, distance).wait_recv()
                    total += z_in[slot, distance - 1].astype(f32)
                mine = window(lot * lot_rows + side * half + place * part, part, 0)
                results[which][mine] = total.astype(bf16)
                for distance in range(1, ways):
                    from_place(which, lot, distance).start()

        def give_across(lot):
            for which in range(2):
                for distance in range(1, ways):
                    from_place(which, lot, distance).wait_recv()
                back_over_x(which, lot).start()

        start_lot(0)
        start_lot(1)
        total_ref[...] = jnp.zeros_like(total_ref)
        rows_ref[...] = jnp.concatenate([q_ref[...], g_ref[...]], axis=0).T
        delta_ref[...] = jnp.sum(g_ref[...].astype(f32) * heads_ref[...], axis=0, keepdims=True)
        kv_ref[:keys, :] = far_ref[...]
        kv_ref[keys:, :] = own_ref[...]

        def key_block(step, at):
            span_keys = pl.ds(pl.multiple_of(step * VIEW_TOK + at * bk, bk), bk)
            key_values = kv_ref[span_keys, :]
            key_columns = key_values.T[:HEAD_DIM]
            empty = jnp.zeros((HEAD_DIM, bq), bf16)
            is_key = lax.broadcasted_iota(jnp.int32, (bq, 2 * HEAD_DIM), 1) < HEAD_DIM

            def parts(pair, accum):
                for bit in range(2):
                    span = pl.ds(pl.multiple_of((pair * 2 + bit) * bq, bq), bq)
                    scores = dot(key_values, jnp.concatenate([q_ref[:, span], empty], axis=0))
                    if masked:
                        scores += bias_ref[step]
                    weights = jnp.exp2(scores - norm_ref[:, span])
                    grad_weights = dot(
                        key_values, jnp.concatenate([empty, g_ref[:, span]], axis=0)
                    )
                    grad_scores = (weights * (grad_weights - delta_ref[:, span])).astype(bf16)
                    rows = rows_ref[span, :]
                    none = jnp.zeros_like(rows)
                    accum += dot(weights.astype(bf16), jnp.where(is_key, none, rows))
                    accum += dot(grad_scores, jnp.where(is_key, rows, none))
                    total_ref[:, span] += dot(key_columns, grad_scores)
                return accum

            accum = lax.fori_loop(
                0, count // (2 * bq), parts, jnp.zeros((bk, 2 * HEAD_DIM), f32)
            )
            lane = lax.broadcasted_iota(jnp.int32, accum.shape, 1)
            accum = jnp.where(lane < HEAD_DIM, accum * (1.0 / LOG2E), accum)

            @pl.when(step < steps // 2)
            def _():
                given_ref[span_keys, :] = accum.astype(bf16)

            @pl.when(step >= steps // 2)
            def _():
                rows = pl.ds(pl.multiple_of(step * VIEW_TOK + at * bk - keys, bk), bk)
                pairs_ref[rows, :] = (accum + met_ref[rows, :].astype(f32)).astype(bf16)

        def view_step(step, none):
            @pl.when(step + 2 < steps)
            def _():
                start_lot(step + 2)

            reduce_across(step)

            @pl.when(step >= 1)
            def _():
                reduce_places(step - 1)

            @pl.when(step >= 2)
            def _():
                give_across(step - 2)

            @pl.when(step >= steps // 2)
            def _():
                far_pairs(step - steps // 2).wait_recv()

            def blocks(at, none):
                key_block(step, at)
                return none

            lax.fori_loop(0, VIEW_TOK // bk, blocks, 0)

            @pl.when(step < steps // 2)
            def _():
                far_pairs(step).start()

            return none

        lax.fori_loop(0, steps, view_step, 0)
        reduce_places(steps - 1)
        give_across(steps - 2)
        out_ref[...] = (total_ref[...] * HEAD_DIM ** (-0.5)).astype(bf16)
        give_across(steps - 1)

        def finish(lot, none):
            for which in range(2):
                over_x(which, lot).wait_send()
                back_over_x(which, lot).wait_recv()
                back_over_x(which, lot).wait_send()
                for distance in range(1, ways):
                    to_places(which, lot, distance).wait_send()
                    from_place(which, lot, distance).wait_send()

            return none

        lax.fori_loop(0, steps, finish, 0)
        for view in range(steps // 2):
            far_pairs(view).wait_send()

    vmem = pl.BlockSpec(memory_space=pltpu.VMEM)
    operands = [q_cols, g_cols, heads_out, kv_far, kv_own, log_norm] + list(grads)
    in_specs = [vmem] * len(operands)
    if bias is not None:
        operands = [bias] + operands
        in_specs = [pl.BlockSpec(memory_space=pltpu.SMEM)] + in_specs
    lots = 2 * steps
    scratch = [
        pltpu.VMEM((HEAD_DIM, count), f32),
        pltpu.VMEM((count, 2 * HEAD_DIM), bf16),
        pltpu.VMEM((1, count), f32),
        pltpu.VMEM((2 * keys, 2 * HEAD_DIM), bf16),
        pltpu.VMEM((keys, 2 * HEAD_DIM), bf16),
        pltpu.VMEM((keys, 2 * HEAD_DIM), bf16),
        pltpu.VMEM((lots, half, width), bf16),
        pltpu.VMEM((lots, half, width), bf16),
        pltpu.VMEM((lots, ways - 1, part, width), bf16),
    ]
    for number_of in (lots, lots * ways, lots * ways, lots, steps // 2):
        scratch += [pltpu.SemaphoreType.DMA((number_of,))] * 2
    return pl.pallas_call(
        kernel,
        in_specs=in_specs,
        out_specs=[vmem] * 4,
        out_shape=[
            jax.ShapeDtypeStruct((keys, 2 * HEAD_DIM), bf16),
            jax.ShapeDtypeStruct((HEAD_DIM, count), bf16),
        ]
        + [jax.ShapeDtypeStruct(grad.shape, bf16) for grad in grads],
        scratch_shapes=scratch,
        compiler_params=pltpu.CompilerParams(
            collective_id=number, has_side_effects=True, vmem_limit_bytes=VMEM_BYTES
        ),
        cost_estimate=pl.CostEstimate(
            flops=80 * HEAD_DIM * count * keys,
            bytes_accessed=20 << 20,
            transcendentals=2 * count * keys,
        ),
    )(*operands)


def last_sums(number, ways, grads, far_part, own_part, small, normed, inverse, gain, resid, mixed):
    chunks = []
    for index, grad in enumerate(grads):
        rows = grad.shape[0] * LOT // grad.size
        chunks += [(index, first, rows) for first in range(0, grad.shape[0], rows)]
    lots = len(chunks)
    rounds = 5

    def kernel(*refs):
        count = len(grads)
        sources = refs[:count]
        far_ref, own_ref, small_ref, normed_ref, inverse_ref, gain_ref, resid_ref, mixed_ref = refs[
            count : count + 8
        ]
        refs = refs[count + 8 :]
        results = refs[:count]
        tokens_ref, mixed_out_ref, small_sum_ref = refs[count : count + 3]
        refs = refs[count + 3 :]
        x_in, x_sums, z_in = refs[:lots], refs[lots : 2 * lots], refs[2 * lots : 3 * lots]
        core_in, pair_ref, chip_in, small_in, small_out = refs[3 * lots : 3 * lots + 5]
        sems = refs[3 * lots + 5 :]
        position = lax.axis_index("dp")
        slot = lax.axis_index("tensor")
        place = position % (2 * ways) // 2
        side = position % 2
        base = position - 2 * place
        across = {"dp": position + 1 - 2 * side}
        places = [lax.rem(place + distance, ways) for distance in range(ways)]
        peers = [{"dp": base + 2 * at} for at in places]
        partner = slot + 1 - 2 * lax.rem(slot, 2)
        chip = lax.rem(slot + 2, 4)
        core_to, chip_to = {"tensor": partner}, {"tensor": chip}
        even = place + 1 - 2 * lax.rem(place, 2)
        steps = [
            core_to,
            chip_to,
            across,
            {"dp": base + 2 * even},
            {"dp": base + 2 * lax.rem(place + 2, ways)},
        ]
        greet([across, core_to, chip_to] + peers[1:])
        pending = []

        def send(source, target, pair, at, to):
            copy = pltpu.make_async_remote_copy(
                src_ref=source,
                dst_ref=target,
                send_sem=sems[2 * pair].at[at],
                recv_sem=sems[2 * pair + 1].at[at],
                device_id=to,
                device_id_type=MESH,
            )
            copy.start()
            pending.append(copy)
            return copy

        mine_first = lax.rem(slot, 2) * own_ref.shape[0]
        own_rows = window(mine_first, own_ref.shape[0], 0)
        small_copy = send(small_ref, small_in.at[0], 1, 0, steps[0])
        core_copy = send(far_ref, core_in, 0, 0, core_to)
        across_copies = []

        def start_across(lot):
            index, first, rows = chunks[lot]
            half = rows // 2
            given = window(first + (1 - side) * half, half, 0)
            across_copies.append(send(sources[index].at[given], x_in[lot], 2, lot, across))

        for lot in range(3):
            start_across(lot)

        def small_round(at, copy):
            copy.wait_recv()
            total = (small_ref if at == 0 else small_out.at[at - 1])[...] + small_in[at]
            if at == rounds - 1:
                small_sum_ref[...] = total
                return None
            small_out[at] = total
            return send(small_out.at[at], small_in.at[at + 1], 1, at + 1, steps[at + 1])

        def reduce_across(lot):
            index, first, rows = chunks[lot]
            half, part = rows // 2, rows // 2 // ways
            across_copies[lot].wait_recv()
            kept = sources[index][window(first + side * half, half, 0)]
            x_sums[lot][...] = (kept.astype(f32) + x_in[lot][...].astype(f32)).astype(bf16)
            return [
                send(
                    x_sums[lot].at[window(places[distance] * part, part, 0)],
                    z_in[lot].at[distance - 1],
                    3,
                    lot * ways + distance,
                    peers[distance],
                )
                for distance in range(1, ways)
            ]

        def reduce_places(lot, copies):
            index, first, rows = chunks[lot]
            half, part = rows // 2, rows // 2 // ways
            total = x_sums[lot][window(place * part, part, 0)].astype(f32)
            for distance in range(1, ways):
                copies[distance - 1].wait_recv()
                total += z_in[lot][distance - 1].astype(f32)
            mine = window(first + side * half + place * part, part, 0)
            results[index][mine] = total.astype(bf16)
            return [
                send(
                    results[index].at[mine],
                    results[index].at[mine],
                    4,
                    lot * ways + distance,
                    peers[distance],
                )
                for distance in range(1, ways)
            ]

        def give_across(lot, copies):
            index, first, rows = chunks[lot]
            half = rows // 2
            for copy in copies:
                copy.wait_recv()
            mine = window(first + side * half, half, 0)
            return send(results[index].at[mine], results[index].at[mine], 5, lot, across)

        small_copy = small_round(0, small_copy)
        core_copy.wait_recv()
        pair_ref[...] = (own_ref[...] + core_in[...].astype(f32)).astype(bf16)
        chip_copy = send(pair_ref, chip_in, 6, 0, chip_to)
        mixed_copy = send(mixed_ref, mixed_out_ref.at[own_rows], 7, 0, core_to)
        mixed_own = pltpu.make_async_copy(mixed_ref, mixed_out_ref.at[own_rows], sems[-1].at[0])
        mixed_own.start()
        small_copy = small_round(1, small_copy)
        reduced, gathered, given = {}, {}, {}
        for step in range(lots + 4):
            if step + 3 < lots:
                start_across(step + 3)
            if step < lots:
                reduced[step] = reduce_across(step)
            if 2 <= step < lots + 2:
                gathered[step - 2] = reduce_places(step - 2, reduced[step - 2])
            if step >= 4:
                given[step - 4] = give_across(step - 4, gathered[step - 4])
            if step in (5, 9):
                small_copy = small_round(2 if step == 5 else 3, small_copy)
        chip_copy.wait_recv()
        strip = 64

        def norm_rows(at, none):
            first = pl.multiple_of(at * strip, strip)
            rows = pl.ds(first, strip)
            grad_norm = pair_ref[rows, :].astype(f32) + chip_in[rows, :].astype(f32)
            scaled = grad_norm * gain_ref[...]
            normed_rows = normed_ref[rows, :]
            grad_input = inverse_ref[rows, :] * (
                scaled
                - jnp.mean(scaled, axis=-1, keepdims=True)
                - normed_rows * jnp.mean(scaled * normed_rows, axis=-1, keepdims=True)
            )
            tokens_ref[pl.ds(pl.multiple_of(mine_first + first, strip), strip), :] = (
                resid_ref[rows, :] + grad_input
            ).astype(bf16)
            return none

        lax.fori_loop(0, own_ref.shape[0] // strip, norm_rows, 0)
        tokens_copy = send(tokens_ref.at[own_rows], tokens_ref.at[own_rows], 8, 0, core_to)
        small_round(4, small_copy)
        mixed_own.wait()
        mixed_copy.wait_recv()
        tokens_copy.wait_recv()
        for lot in range(lots):
            given[lot].wait_recv()
        for copy in pending:
            copy.wait_send()

    vmem = pl.BlockSpec(memory_space=pltpu.VMEM)
    shapes = [jax.ShapeDtypeStruct(grad.shape, bf16) for grad in grads]
    both = jax.ShapeDtypeStruct((2 * own_part.shape[0], own_part.shape[1]), bf16)
    shapes += [both, both, jax.ShapeDtypeStruct(small.shape, f32)]
    wide = [grads[index].shape[1] for index, _, _ in chunks]
    scratch = [pltpu.VMEM((lot[2] // 2, w), bf16) for lot, w in zip(chunks, wide)]
    scratch += [pltpu.VMEM((lot[2] // 2, w), bf16) for lot, w in zip(chunks, wide)]
    scratch += [pltpu.VMEM((ways - 1, lot[2] // 2 // ways, w), bf16) for lot, w in zip(chunks, wide)]
    scratch += [pltpu.VMEM(far_part.shape, bf16)] * 3
    scratch += [pltpu.VMEM((rounds,) + small.shape, f32)] * 2
    for number_of in (1, rounds, lots, lots * ways, lots * ways, lots, 1, 1, 1):
        scratch += [pltpu.SemaphoreType.DMA((number_of,))] * 2
    scratch.append(pltpu.SemaphoreType.DMA((1,)))
    return pl.pallas_call(
        kernel,
        in_specs=[vmem] * (len(grads) + 8),
        out_specs=[vmem] * len(shapes),
        out_shape=shapes,
        scratch_shapes=scratch,
        compiler_params=pltpu.CompilerParams(
            collective_id=number, has_side_effects=True, vmem_limit_bytes=44 << 20
        ),
        cost_estimate=pl.CostEstimate(flops=0, bytes_accessed=150 << 20, transcendentals=0),
    )(*grads, far_part, own_part, small, normed, inverse, gain, resid, mixed)


def shards(
    tokens,
    views,
    ln1_gain,
    ln1_bias,
    w_query,
    w_key,
    w_value,
    w_out,
    ln2_gain,
    ln2_bias,
    w_up,
    w_down,
    cotangent,
):
    row_count, width = tokens.shape
    inner = w_query.shape[1]
    heads = inner // HEAD_DIM
    half = row_count // 2
    group = MAX_VIEWS * VIEW_TOK // row_count
    devices = lax.axis_size("dp")
    assert row_count == VIEW_TOK and group == 2 * heads and lax.axis_size("tensor") == 4
    position = lax.axis_index("dp")
    block = position % group
    side = block % 2
    core = lax.axis_index("tensor") % 2
    scene_views = lax.dynamic_index_in_dim(views, position // group, keepdims=False)
    own_views = ((scene_views + 1 - side) // 2).reshape(1)
    far_views = ((scene_views + side) // 2).reshape(1)
    keep = (block < scene_views).astype(f32)
    def across(block):
        return lax.ppermute(block, "dp", [(i, i ^ 1) for i in range(devices)])

    def other_core(block):
        return lax.ppermute(block, "tensor", [(i, i ^ 1) for i in range(4)])

    def other_chip(block):
        return lax.ppermute(block, "tensor", [(i, i ^ 2) for i in range(4)])

    def own_first(block):
        return jnp.where(core == 0, block, jnp.concatenate([block[half:], block[:half]], axis=0))

    def pair_sum(far_part, own_part):
        arrived = other_core(far_part.astype(bf16))
        return (own_part + arrived.astype(f32)).astype(bf16)

    def both_halves(own):
        return jnp.concatenate([own, other_core(own)], axis=0)

    grad_rows = own_first(cotangent)
    inputs_own = jnp.where(core == 0, tokens[:half], tokens[half:]).astype(f32)
    grad_own = grad_rows[:half].astype(f32)

    attn_in, normed_first, inverse_first = first_norm(core, tokens, ln1_gain, ln1_bias)
    w_pairs = jnp.concatenate(
        [w_key.reshape(width, heads, HEAD_DIM), w_value.reshape(width, heads, HEAD_DIM)], axis=2
    ).reshape(width, 2 * inner)
    kv_low = dot(attn_in, w_pairs).astype(bf16)
    query_low = (contract(w_query, attn_in, 0, 1) * (LOG2E * HEAD_DIM ** (-0.5))).astype(bf16)
    q_cols, kv_own = exchange(1, heads, (query_low, 0, 1), (kv_low, 1, 0))
    kv_far = across(kv_own)

    carry = sweep_forward(own_views, q_cols, kv_own, None, False)
    heads_out, heads_low, log_norm = sweep_forward(far_views, q_cols, kv_far, carry, True)
    (attn_cols,) = exchange(2, heads, (heads_low, 1, 0))

    pair = pair_sum(
        contract(attn_cols[:, half:], w_out, 0, 0), contract(attn_cols[:, :half], w_out, 0, 0)
    )
    resid = inputs_own + keep * (pair.astype(f32) + other_chip(pair).astype(f32))
    mlp_norm, normed_second, inverse_second = layer_norm(resid, ln2_gain, ln2_bias)
    mlp_in = both_halves(mlp_norm.astype(bf16))
    grad_mlp = (keep * grad_rows.astype(f32)).astype(bf16)
    grad_act = lax.optimization_barrier(contract(grad_mlp, w_down, 1, 1))
    up_proj = dot(mlp_in, w_up)
    activated, gelu_pull = jax.vjp(partial(jax.nn.gelu, approximate=True), up_proj)
    act_low = activated.astype(bf16)
    grad_up = gelu_pull(grad_act)[0].astype(bf16)
    pair = pair_sum(contract(grad_up[half:], w_up, 1, 1), contract(grad_up[:half], w_up, 1, 1))
    w_down_grad = contract(act_low, grad_mlp, 0, 0).astype(bf16)
    w_up_grad = contract(mlp_in, grad_up, 0, 0).astype(bf16)
    arrived, act_low, w_up_grad, w_down_grad = lax.optimization_barrier(
        (other_chip(pair), act_low, w_up_grad, w_down_grad)
    )
    grad_mlp_in = pair.astype(f32) + arrived.astype(f32)
    mlp_pair = pair_sum(dot(act_low[half:], w_down), dot(act_low[:half], w_down))
    mlp_arrived = other_chip(mlp_pair)
    grad_second, ln2_gain_grad, ln2_bias_grad = norm_back(
        grad_mlp_in, normed_second, inverse_second, ln2_gain
    )
    grad_resid = grad_own + grad_second
    grad_attn = both_halves((keep * grad_resid).astype(bf16))
    grad_heads = contract(w_out, grad_attn, 1, 1).astype(bf16)
    (g_cols,) = exchange(3, heads, (grad_heads, 0, 1))
    w_out_grad = dot(attn_cols, grad_attn).astype(bf16)

    bias = None
    if devices > group:
        seen = 2 * jnp.arange(heads, dtype=jnp.int32)
        seen = jnp.concatenate([seen + 1 - side, seen + side])
        bias = jnp.where(seen < scene_views, 0.0, -1e30).astype(f32)
    pairs, dq_cols, w_up_grad, w_down_grad = sweep_backward(
        6,
        heads,
        bias,
        q_cols,
        g_cols,
        heads_out,
        kv_far,
        kv_own,
        log_norm,
        (w_up_grad, w_down_grad),
    )
    resid, mlp_pair, mlp_arrived, pairs = lax.optimization_barrier(
        (resid, mlp_pair, mlp_arrived, pairs)
    )
    mixed_own = (
        resid + keep * (mlp_pair.astype(f32) + mlp_arrived.astype(f32))
    ).astype(bf16)
    grad_query, grad_pairs = exchange(4, heads, (dq_cols, 1, 0), (pairs, 0, 1))

    def partial_in(start):
        return contract(grad_query[:, start : start + half], w_query, 0, 1) + contract(
            grad_pairs[start : start + half], w_pairs, 1, 1
        )

    far_part, own_part = partial_in(half), partial_in(0)
    small = jnp.stack(
        [
            jnp.sum(far_part * normed_first[half:], axis=0)
            + jnp.sum(own_part * normed_first[:half], axis=0),
            jnp.sum(far_part, axis=0) + jnp.sum(own_part, axis=0),
            ln2_gain_grad * 0.5,
            ln2_bias_grad * 0.5,
        ]
        + [jnp.zeros((width,), f32)] * 4
    )
    late = (
        w_out_grad,
        contract(attn_in, grad_pairs, 0, 0).astype(bf16),
        contract(attn_in, grad_query, 0, 1).astype(bf16),
    )
    w_out_grad, w_pairs_grad, w_query_grad, tokens_grad, mixed, small = last_sums(
        5,
        heads,
        late,
        far_part.astype(bf16),
        own_part,
        small,
        normed_first[:half],
        inverse_first[:half],
        ln1_gain.reshape(1, width),
        grad_resid,
        mixed_own,
    )
    if devices > group:
        same = [list(range(at, devices, group)) for at in range(group)]
        w_out_grad, w_pairs_grad, w_query_grad, w_up_grad, w_down_grad, small = [
            lax.psum(array, "dp", axis_index_groups=same)
            for array in (
                w_out_grad,
                w_pairs_grad,
                w_query_grad,
                w_up_grad,
                w_down_grad,
                small,
            )
        ]
    w_pairs_grad = w_pairs_grad.astype(f32).reshape(width, heads, 2 * HEAD_DIM)

    return (
        mixed,
        tokens_grad,
        small[0],
        small[1],
        w_query_grad.astype(f32),
        w_pairs_grad[:, :, :HEAD_DIM].reshape(width, inner),
        w_pairs_grad[:, :, HEAD_DIM:].reshape(width, inner),
        w_out_grad.astype(f32),
        small[2],
        small[3],
        w_up_grad.astype(f32),
        w_down_grad.astype(f32),
    )


def solution(mesh):
    placed = (
        P("dp", None),
        P(),
        P(),
        P(),
        P(None, "tensor"),
        P(None, "tensor"),
        P(None, "tensor"),
        P("tensor", None),
        P(),
        P(),
        P(None, "tensor"),
        P("tensor", None),
        P("dp", None),
    )
    return jax.shard_map(
        shards,
        mesh=mesh,
        in_specs=placed,
        out_specs=(
            P("dp", None),
            P("dp", None),
            P(),
            P(),
            P(None, "tensor"),
            P(None, "tensor"),
            P(None, "tensor"),
            P("tensor", None),
            P(),
            P(),
            P(None, "tensor"),
            P("tensor", None),
        ),
        check_vma=False,
    )
```

profile of v0, /device:TPU:0, one launch (start us, length us, event | category | flops | bytes accessed | tf_op | source)
XLA Modules:
  0.0 478.8 jit_solution(11811339182608880169)
XLA Ops:
  0.7 2.2 copy.28
  2.9 2.0 copy.29
  4.9 1.3 pad_maximum_fusion.12
  6.2 5.8 %shard_map.220 = (bf16[1024,1024]{1,0:T(8,128)(2,1)}, f32[1024,1024]{1,0:T(8,128)}, f32[1024,1]{1,0:T(8,128)}) custom-call(s32[1]{0:T(128)} %bitcast.2.core_ref, bf16[1024,1024]{1,0:T(8,128)(2,1)} %tokens_ref.1, f32[1,1024]{1,0:T(1,128)} %bitcast.51, f32[1,1024]{1,0:T(1,128)} %bitcast.65), custom_call_target="tpu_custom_call" | custom-call | flops 10485760 | bytes 8388608 | tf_op jit(solution)/shard_map/pallas_call | solution.py:63
  12.0 2.6 fusion.17.refs_0_
  14.6 1.3 convolution_convert_fusion.6.refs_1_
  15.9 31.6 %shard_map.221 = (bf16[64,4096]{1,0:T(8,128)(2,1)S(1)}, bf16[4096,128]{1,0:T(8,128)(2,1)S(1)}) custom-call(bf16[256,1024]{1,0:T(8,128)(2,1)S(1)} %fusion.17.refs_0_, bf16[1024,512]{1,0:T(8,128)(2,1)S(1)} %convolution_convert_fusion.6.refs_1_), custom_call_target="tpu_custom_call" | custom-call | bytes 62914560 | tf_op jit(solution)/shard_map/pallas_call | solution.py:226
  48.3 1.5 collective-permute-start
  51.5 21.7 %shard_map.222 = (f32[1,4096]{1,0:T(1,128)S(1)}, f32[80,4096]{1,0:T(8,128)S(1)}) custom-call(s32[1]{0:T(128)} %bitcast.9.refs_0_, bf16[64,4096]{1,0:T(8,128)(2,1)S(1)} %copy-done.12, bf16[4096,128]{1,0:T(8,128)(2,1)S(1)} %get-tuple-element.44.refs_2_.refs_4_), custom_call_target="tpu_custom_call" | custom-call | flops 17179869184 | bytes 8388608 | tf_op jit(solution)/shard_map/pallas_call | solution.py:148
  73.4 26.4 %shard_map.223 = (f32[64,4096]{1,0:T(8,128)S(1)}, bf16[64,4096]{1,0:T(8,128)(2,1)S(1)}, f32[1,4096]{1,0:T(1,128)S(1)}) custom-call(s32[1]{0:T(128)} %bitcast.1.refs_0_, bf16[64,4096]{1,0:T(8,128)(2,1)S(1)} %copy-done.12, bf16[4096,128]{1,0:T(8,128)(2,1)} %collective-permute-done.refs_2_.refs_3_, f32[1,4096]{1,0:T(1,128)S(1)} %get-tuple-element.45.refs_3_, ...), custom_call_target="tpu_custom_call" | custom-call | flops 17179869184 | bytes 8388608 | tf_op jit(solution)/shard_map/pallas_call | solution.py:148
  99.8 20.2 %shard_map.224 = bf16[256,1024]{1,0:T(8,128)(2,1)S(1)} custom-call(bf16[64,4096]{1,0:T(8,128)(2,1)S(1)} %get-tuple-element.47.refs_0_), custom_call_target="tpu_custom_call" | custom-call | bytes 20971520 | tf_op jit(solution)/shard_map/pallas_call | solution.py:226
  120.6 2.6 collective-permute-done.1
  123.2 1.4 add_convert_fusion.4
  124.7 1.5 collective-permute-start.2
  126.2 24.0 %collective-permute-done.2 = bf16[512,1024]{1,0:T(8,128)(2,1)} collective-permute-done((bf16[512,1024]{1,0:T(8,128)(2,1)}, bf16[512,1024]{1,0:T(8,128)(2,1)}, u32[]{:S(2)}, u32[]{:S(2)}) %collective-permute-start.2) | collective-permute-done | bytes 1048608 | tf_op jit(solution)/shard_map/ppermute | solution.py:717
  150.2 2.9 fusion.38
  156.8 2.4 fusion.9
  159.2 6.6 %multiply_convert_fusion = (bf16[1024,1024]{1,0:T(8,128)(2,1)S(1)}, bf16[1024,1024]{1,0:T(8,128)(2,1)S(1)}) fusion(f32[1024,1024]{1,0:T(8,128)S(1)} %fusion.9, bf16[1024,1024]{1,0:T(8,128)(2,1)S(1)} %copy-done, bf16[512,1024]{1,0:T(8,128)(2,1)S(1)} %collective-permute-done.3, bf16[512,1024]{1,0:T(8,128)(2,1)S(1)} %add_convert_fusion.3), kind=kOutput, calls=%fused_computation.9 | convolution fusion | flops 2174746624 | bytes 12582912 | tf_op jit(solution)/shard_map/dot_general | solution.py:754
  165.8 1.3 convolution_convert_fusion.4
  167.1 2.6 collective-permute-done.4
  169.8 1.3 add_convert_fusion.2
  171.1 1.6 collective-permute-start.5
  172.7 3.7 convolution_convert_fusion.1.refs_6_
  176.4 3.7 convolution_convert_fusion.refs_7_
  180.1 16.3 %collective-permute-done.5 = bf16[512,1024]{1,0:T(8,128)(2,1)S(1)} collective-permute-done((bf16[512,1024]{1,0:T(8,128)(2,1)S(1)}, bf16[512,1024]{1,0:T(8,128)(2,1)S(1)}, u32[]{:S(2)}, u32[]{:S(2)}) %collective-permute-start.5) | collective-permute-done | bytes 1048608 | tf_op jit(solution)/shard_map/ppermute | solution.py:717
  197.4 1.3 convolution_convert_fusion.3
  198.8 2.3 multiply_convert_fusion.2
  201.6 1.3 add_convert_fusion.1
  202.9 1.6 collective-permute-start.8
  205.3 13.8 %shard_map.225.refs_1_ = bf16[64,4096]{1,0:T(8,128)(2,1)S(1)} custom-call(bf16[256,1024]{1,0:T(8,128)(2,1)S(1)} %fusion.18.refs_0_), custom_call_target="tpu_custom_call" | custom-call | bytes 20971520 | tf_op jit(solution)/shard_map/pallas_call | solution.py:226
  219.1 124.9 %shard_map.226 = (bf16[4096,128]{1,0:T(8,128)(2,1)S(1)}, bf16[64,4096]{1,0:T(8,128)(2,1)S(1)}, bf16[1024,1024]{1,0:T(8,128)(2,1)}, bf16[1024,1024]{1,0:T(8,128)(2,1)}) custom-call(bf16[64,4096]{1,0:T(8,128)(2,1)S(1)} %copy-done.13, bf16[64,4096]{1,0:T(8,128)(2,1)S(1)} %shard_map.225.refs_1_, f32[64,4096]{1,0:T(8,128)S(1)} %copy-done.15, ...), custom_call_target="tpu_custom_call" | custom-call | flops 85899345920 | bytes 20971520 | tf_op jit(solution)/shard_map/pallas_call | solution.py:458
  344.0 4.2 convert_element_type.157
  348.3 2.5 convert_element_type.158
  350.7 1.5 fusion.14.refs_0_
  352.3 26.7 %shard_map.227 = (bf16[256,1024]{1,0:T(8,128)(2,1)S(1)}, bf16[1024,512]{1,0:T(8,128)(2,1)S(1)}) custom-call(bf16[64,4096]{1,0:T(8,128)(2,1)S(1)} %get-tuple-element.53.refs_0_, bf16[4096,128]{1,0:T(8,128)(2,1)S(1)} %get-tuple-element.56.refs_1_), custom_call_target="tpu_custom_call" | custom-call | bytes 62914560 | tf_op jit(solution)/shard_map/pallas_call | solution.py:226
  378.9 1.6 convolution_convert_fusion.7.refs_2_
  381.5 1.3 convolution_convert_fusion.2.refs_1_
  383.6 2.2 copy-done.24
  385.7 2.5 multiply_reduce_fusion.1
  391.1 72.1 %shard_map.228 = (bf16[256,1024]{1,0:T(8,128)(2,1)S(1)}, bf16[1024,512]{1,0:T(8,128)(2,1)S(1)}, bf16[1024,256]{1,0:T(8,128)(2,1)S(1)}, bf16[1024,1024]{1,0:T(8,1...) custom-call(bf16[256,1024]{1,0:T(8,128)(2,1)S(1)} %copy-done.6, ...), custom_call_target="tpu_custom_call" | custom-call | bytes 157286400 | tf_op jit(solution)/shard_map/pallas_call | solution.py:667
  463.2 1.3 copy-done.2
  466.1 1.0 convert_element_type.155
  467.1 1.1 convert_element_type.156
  468.8 1.2 fusion.39
  469.9 2.5 copy.34
  472.5 1.3 copy.33
  473.8 3.2 copy.41
  477.0 1.3 copy.42
  (100 shorter events, 15.3 us)
Async XLA Ops:
  0.6 158.5 %copy-start = (bf16[1024,1024]{1,0:T(8,128)(2,1)S(1)}, bf16[1024,1024]{1,0:T(8,128)(2,1)}, u32[]{:S(2)}) copy-start(bf16[1024,1024]{1,0:T(8,128)(2,1)} %param.23) | copy-start | bytes 6291460
  6.2 8.4 %copy-start.17 = (bf16[1024,4,128]{0,2,1:T(8,128)(2,1)}, bf16[1024,4,128]{0,2,1:T(8,128)(2,1)S(1)}, u32[]{:S(2)}) copy-start(bf16[1024,4,128]{0,2,1:T(8,128)(2,1)S(1)} %pad_maximum_fusion.12) | copy-start | bytes 3145732
  12.0 2.6 copy-start.33
  47.5 0.8 copy-start.11
  48.3 25.0 %copy-start.9 = (bf16[4096,128]{1,0:T(8,128)(2,1)}, bf16[4096,128]{1,0:T(8,128)(2,1)S(1)}, u32[]{:S(2)}) copy-start(bf16[4096,128]{1,0:T(8,128)(2,1)S(1)} %get-tuple-element.44.refs_2_.refs_4_) | copy-start | bytes 3145732
  48.3 25.1 %collective-permute-start = (bf16[4096,128]{1,0:T(8,128)(2,1)S(1)}, bf16[4096,128]{1,0:T(8,128)(2,1)}, u32[]{:S(2)}, u32[]{:S(2)}) collective-permute-start(bf16[4096,128]{1,0:T(8,128)(2,1)S(1)} %get-tuple-element.44.refs_2_.refs_4_), channel_id=1, source_target_pairs={{0,4},{4,0},{8,12},{12,8},{16,20},{20,16},{24,28},{28,24},{1,5},{5... | collective-permute-start | bytes 3145736 | tf_op jit(solution)/shard_map/ppermute | solution.py:711
  50.5 1.0 copy-start.12
  73.4 46.6 %copy-start.21 = (bf16[256,1024]{1,0:T(8,128)(2,1)S(1)}, bf16[256,1024]{1,0:T(8,128)(2,1)}, u32[]{:S(2)}) copy-start(bf16[256,1024]{1,0:T(8,128)(2,1)} %param.20) | copy-start | bytes 1572868
  99.8 24.9 %copy-start.14 = (f32[64,4096]{1,0:T(8,128)}, f32[64,4096]{1,0:T(8,128)S(1)}, u32[]{:S(2)}) copy-start(f32[64,4096]{1,0:T(8,128)S(1)} %get-tuple-element.49.refs_2_) | copy-start | bytes 3145732
  120.5 2.7 collective-permute-start.1
  124.7 25.5 %collective-permute-start.2 = (bf16[512,1024]{1,0:T(8,128)(2,1)}, bf16[512,1024]{1,0:T(8,128)(2,1)}, u32[]{:S(2)}, u32[]{:S(2)}) collective-permute-start(bf16[512,1024]{1,0:T(8,128)(2,1)} %add_convert_fusion.4), channel_id=1, source_target_pairs={{0,2},{1,3},{2,0},{3,1},{4,6},{5,7},{6,4},{7,5},{8,10},{9,11},{10,... | collective-permute-start | bytes 3145736 | tf_op jit(solution)/shard_map/ppermute | solution.py:717
  153.0 0.7 copy-start.30
  153.0 0.7 copy-start.31
  153.4 1.6 copy-start.19
  154.2 5.0 %collective-permute-start.3 = (bf16[512,1024]{1,0:T(8,128)(2,1)S(1)}, bf16[512,1024]{1,0:T(8,128)(2,1)S(1)}, u32[]{:S(2)}, u32[]{:S(2)}) collective-permute-start(bf16[512,1024]{1,0:T(8,128)(2,1)S(1)} %add_convert_fusion.3), channel_id=1, source_target_pairs={{0,1},{1,0},{2,3},{3,2},{4,5},{5,4},{6,7},{7,6},{8,9},{9,8},{10,11... | collective-permute-start | bytes 3145736 | tf_op jit(solution)/shard_map/ppermute | solution.py:714
  155.2 1.6 copy-start.32
  167.1 2.7 collective-permute-start.4
  171.1 25.3 %collective-permute-start.5 = (bf16[512,1024]{1,0:T(8,128)(2,1)S(1)}, bf16[512,1024]{1,0:T(8,128)(2,1)S(1)}, u32[]{:S(2)}, u32[]{:S(2)}) collective-permute-start(bf16[512,1024]{1,0:T(8,128)(2,1)S(1)} %add_convert_fusion.2), channel_id=1, source_target_pairs={{0,2},{1,3},{2,0},{3,1},{4,6},{5,7},{6,4},{7,5},{8,10},{9,11},{10,... | collective-permute-start | bytes 3145736 | tf_op jit(solution)/shard_map/ppermute | solution.py:717
  198.7 3.0 collective-permute-start.7
  198.7 2.8 copy-start.29
  201.1 3.4 collective-permute-start.6
  201.6 2.9 copy-start.22
  202.9 2.4 copy-start.25
  202.9 16.2 %copy-start.10 = (bf16[4096,128]{1,0:T(8,128)(2,1)S(1)}, bf16[4096,128]{1,0:T(8,128)(2,1)}, u32[]{:S(2)}) copy-start(bf16[4096,128]{1,0:T(8,128)(2,1)} %copy-done.9) | copy-start | bytes 3145732
  202.9 16.2 %copy-start.13 = (bf16[64,4096]{1,0:T(8,128)(2,1)S(1)}, bf16[64,4096]{1,0:T(8,128)(2,1)}, u32[]{:S(2)}) copy-start(bf16[64,4096]{1,0:T(8,128)(2,1)} %copy-done.11) | copy-start | bytes 1572868
  202.9 16.2 %copy-start.15 = (f32[64,4096]{1,0:T(8,128)S(1)}, f32[64,4096]{1,0:T(8,128)}, u32[]{:S(2)}) copy-start(f32[64,4096]{1,0:T(8,128)} %copy-done.14) | copy-start | bytes 3145732
  202.9 149.3 %collective-permute-start.8 = (bf16[512,1024]{1,0:T(8,128)(2,1)S(1)}, bf16[512,1024]{1,0:T(8,128)(2,1)S(1)}, u32[]{:S(2)}, u32[]{:S(2)}) collective-permute-start(bf16[512,1024]{1,0:T(8,128)(2,1)S(1)} %add_convert_fusion.1), channel_id=1, source_target_pairs={{0,2},{1,3},{2,0},{3,1},{4,6},{5,7},{6,4},{7,5},{8,10},{9,11},{10,... | collective-permute-start | bytes 3145736 | tf_op jit(solution)/shard_map/ppermute | solution.py:717
  344.0 4.2 copy-start.20
  350.7 28.2 %copy-start.34 = (bf16[1024,1024]{1,0:T(8,128)(2,1)S(1)}, bf16[1024,1024]{1,0:T(8,128)(2,1)}, u32[]{:S(2)}) copy-start(bf16[1024,1024]{1,0:T(8,128)(2,1)} %get-tuple-element.42) | copy-start | bytes 6291460
  352.3 28.2 %copy-start.27 = (bf16[512,1024]{1,0:T(8,128)(2,1)}, bf16[512,1024]{1,0:T(8,128)(2,1)S(1)}, u32[]{:S(2)}) copy-start(bf16[512,1024]{1,0:T(8,128)(2,1)S(1)} %collective-permute-done.8) | copy-start | bytes 3145732
  378.9 1.6 copy-start.23
  381.5 1.3 copy-start.18
  382.8 2.9 copy-start.24
  383.6 4.7 copy-start.16
  385.7 2.5 copy-start.26
  385.7 2.6 copy-start.28
  388.3 0.7 copy-start.8
  389.0 1.0 copy-start.6
  390.0 1.0 copy-start.7
  463.2 1.3 copy-start.2
  464.5 1.0 copy-start.4
  465.5 2.8 copy-start.5
  473.8 3.2 copy-start.3
  473.8 4.6 copy-start.1
where the time goes:
time: 486 us; the launch traced here: 479 us
  Pallas kernels  343 us (71%)
  waiting for transfers between devices  45.7 us (9%)
  matrix products  36.5 us (8%)
  local copies, waits for them, and re-layouts  25.3 us (5%)
  other arithmetic  18.7 us (4%)
  starting transfers between devices  6.94 us (1%)
    pallas_call x1, Pallas kernels, sweep_backward(): pl.pallas_call(kernel, in_specs=in_specs, out_specs=[vmem] * 4, out_shape...  125 us
    pallas_call x4, Pallas kernels, exchange(): pl.pallas_call(kernel, in_specs=[vmem] * count, out_specs=[vmem] * count,...  92.2 us
    pallas_call x1, Pallas kernels, last_sums(): pl.pallas_call(kernel, in_specs=[vmem] * (len(grads) + 8), out_specs=[vme...  72.1 us
    pallas_call x2, Pallas kernels, sweep_forward(): pl.pallas_call(kernel, grid=(count // bq,), in_specs=in_specs, out_specs=...  48.1 us
    ppermute x3, waiting for transfers between devices, other_chip(): return lax.ppermute(block, 'tensor', [(i, i ^ 2) for i in range(4)])  40.3 us
    dot_general x15, matrix products, contract(): lax.dot_general(left, right, (((left_dim,), (right_dim,)), ((), ())), pre...  24.7 us
    unnamed x76, local copies, waits for them, and re-layouts  22.8 us
  transfers between devices with their start and end apart: 9, of which 5 were waited for; matrix products, arithmetic and copies ran while one was open for 5% of the time, Pallas kernels for 34%

commit v1 on v0

--- a/solution.py
+++ b/solution.py
@@ -254,9 +254,10 @@
         bias_ref = refs[0] if masked else None
         refs = refs[1:] if masked else refs
         q_ref, g_ref, heads_ref, far_ref, own_ref, norm_ref = refs[:6]
-        sources, pairs_ref, out_ref, results = refs[6:8], refs[8], refs[9], refs[10:12]
+        sources, home_ref, query_ref, results = refs[6:8], refs[8], refs[9], refs[10:12]
         total_ref, rows_ref, delta_ref, kv_ref, given_ref, met_ref, x_in, x_sums, z_in = refs[12:21]
-        sems = refs[21:]
+        pairs_ref, low_ref = refs[21:23]
+        sems = refs[23:]
         position = lax.axis_index("dp")
         place = position % (2 * ways) // 2
         side = position % 2
@@ -303,6 +304,26 @@
         def far_pairs(view):
             span = window(view * VIEW_TOK, VIEW_TOK, 0)
             return remote(given_ref.at[span], met_ref.at[span], 4, view, across)
+
+        def pairs_home(distance):
+            span = window(lax.rem(place + distance, ways) * VIEW_TOK, VIEW_TOK, 0)
+            return (
+                pairs_ref.at[span],
+                home_ref.at[window(place * 2 * HEAD_DIM, 2 * HEAD_DIM, 1)],
+                5,
+                distance,
+                {"dp": base + 2 * lax.rem(place + distance, ways)},
+            )
+
+        def query_home(distance):
+            span = window(places[distance] * VIEW_TOK, VIEW_TOK, 1)
+            return (
+                low_ref.at[span],
+                query_ref.at[window(place * HEAD_DIM, HEAD_DIM, 0)],
+                6,
+                distance,
+                peers[distance],
+            )
 
         def start_lot(lot):
             for which in range(2):
@@ -343,9 +364,15 @@
         kv_ref[:keys, :] = far_ref[...]
         kv_ref[keys:, :] = own_ref[...]
 
+        def view_of(step):
+            return lax.rem(place + 1 + lax.rem(step, ways), ways)
+
         def key_block(step, at):
-            span_keys = pl.ds(pl.multiple_of(step * VIEW_TOK + at * bk, bk), bk)
-            key_values = kv_ref[span_keys, :]
+            view = view_of(step)
+            own = step // ways
+            first = pl.multiple_of(view * VIEW_TOK + at * bk, bk)
+            rows_here = pl.ds(first, bk)
+            key_values = kv_ref[pl.ds(pl.multiple_of(own * keys + first, bk), bk), :]
             key_columns = key_values.T[:HEAD_DIM]
             empty = jnp.zeros((HEAD_DIM, bq), bf16)
             is_key = lax.broadcasted_iota(jnp.int32, (bq, 2 * HEAD_DIM), 1) < HEAD_DIM
@@ -355,7 +382,7 @@
                     span = pl.ds(pl.multiple_of((pair * 2 + bit) * bq, bq), bq)
                     scores = dot(key_values, jnp.concatenate([q_ref[:, span], empty], axis=0))
                     if masked:
-                        scores += bias_ref[step]
+                        scores += bias_ref[own * ways + view]
                     weights = jnp.exp2(scores - norm_ref[:, span])
                     grad_weights = dot(
                         key_values, jnp.concatenate([empty, g_ref[:, span]], axis=0)
@@ -376,12 +403,11 @@
 
             @pl.when(step < steps // 2)
             def _():
-                given_ref[span_keys, :] = accum.astype(bf16)
+                given_ref[rows_here, :] = accum.astype(bf16)
 
             @pl.when(step >= steps // 2)
             def _():
-                rows = pl.ds(pl.multiple_of(step * VIEW_TOK + at * bk - keys, bk), bk)
-                pairs_ref[rows, :] = (accum + met_ref[rows, :].astype(f32)).astype(bf16)
+                pairs_ref[rows_here, :] = (accum + met_ref[rows_here, :].astype(f32)).astype(bf16)
 
         def view_step(step, none):
             @pl.when(step + 2 < steps)
@@ -400,7 +426,7 @@
 
             @pl.when(step >= steps // 2)
             def _():
-                far_pairs(step - steps // 2).wait_recv()
+                far_pairs(view_of(step)).wait_recv()
 
             def blocks(at, none):
                 key_block(step, at)
@@ -410,15 +436,30 @@
 
             @pl.when(step < steps // 2)
             def _():
-                far_pairs(step).start()
+                far_pairs(view_of(step)).start()
+
+            @pl.when(jnp.logical_and(step >= steps // 2, step < steps - 1))
+            def _():
+                remote(*pairs_home(step + 1 - steps // 2)).start()
 
             return none
 
         lax.fori_loop(0, steps, view_step, 0)
         reduce_places(steps - 1)
+        low_ref[...] = (total_ref[...] * HEAD_DIM ** (-0.5)).astype(bf16)
+        for distance in range(1, ways):
+            remote(*query_home(distance)).start()
+        mine = pltpu.make_async_copy(*pairs_home(0)[:2], sems[-1].at[0])
+        mine.start()
+        mine_too = pltpu.make_async_copy(*query_home(0)[:2], sems[-1].at[1])
+        mine_too.start()
         give_across(steps - 2)
-        out_ref[...] = (total_ref[...] * HEAD_DIM ** (-0.5)).astype(bf16)
         give_across(steps - 1)
+        mine.wait()
+        mine_too.wait()
+        for distance in range(1, ways):
+            remote(*pairs_home(distance)).wait()
+            remote(*query_home(distance)).wait()
 
         def finish(lot, none):
             for which in range(2):
@@ -452,16 +493,19 @@
         pltpu.VMEM((lots, half, width), bf16),
         pltpu.VMEM((lots, half, width), bf16),
         pltpu.VMEM((lots, ways - 1, part, width), bf16),
+        pltpu.VMEM((keys, 2 * HEAD_DIM), bf16),
+        pltpu.VMEM((HEAD_DIM, count), bf16),
     ]
-    for number_of in (lots, lots * ways, lots * ways, lots, steps // 2):
+    for number_of in (lots, lots * ways, lots * ways, lots, steps // 2, ways, ways):
         scratch += [pltpu.SemaphoreType.DMA((number_of,))] * 2
+    scratch.append(pltpu.SemaphoreType.DMA((2,)))
     return pl.pallas_call(
         kernel,
         in_specs=in_specs,
         out_specs=[vmem] * 4,
         out_shape=[
-            jax.ShapeDtypeStruct((keys, 2 * HEAD_DIM), bf16),
-            jax.ShapeDtypeStruct((HEAD_DIM, count), bf16),
+            jax.ShapeDtypeStruct((VIEW_TOK, ways * 2 * HEAD_DIM), bf16),
+            jax.ShapeDtypeStruct((ways * HEAD_DIM, VIEW_TOK), bf16),
         ]
         + [jax.ShapeDtypeStruct(grad.shape, bf16) for grad in grads],
         scratch_shapes=scratch,
@@ -778,7 +822,7 @@
         seen = 2 * jnp.arange(heads, dtype=jnp.int32)
         seen = jnp.concatenate([seen + 1 - side, seen + side])
         bias = jnp.where(seen < scene_views, 0.0, -1e30).astype(f32)
-    pairs, dq_cols, w_up_grad, w_down_grad = sweep_backward(
+    grad_pairs, grad_query, w_up_grad, w_down_grad = sweep_backward(
         6,
         heads,
         bias,
@@ -790,14 +834,12 @@
         log_norm,
         (w_up_grad, w_down_grad),
     )
-    resid, mlp_pair, mlp_arrived, pairs = lax.optimization_barrier(
-        (resid, mlp_pair, mlp_arrived, pairs)
+    resid, mlp_pair, mlp_arrived, grad_query = lax.optimization_barrier(
+        (resid, mlp_pair, mlp_arrived, grad_query)
     )
     mixed_own = (
         resid + keep * (mlp_pair.astype(f32) + mlp_arrived.astype(f32))
     ).astype(bf16)
-    grad_query, grad_pairs = exchange(4, heads, (dq_cols, 1, 0), (pairs, 0, 1))
-
     def partial_in(start):
         return contract(grad_query[:, start : start + half], w_query, 0, 1) + contract(
             grad_pairs[start : start + half], w_pairs, 1, 1

time: 486 us -> 481 us (0.990)
  Pallas kernels: 343 us -> 336 us
    pallas_call x1, Pallas kernels: 125 us -> 152 us  [sweep_backward(): pl.pallas_call(kernel, in_specs=in_specs, out_specs=[vmem] * 4, out_shape...]
    pallas_call x4 -> x3, Pallas kernels: 92.2 us -> 65.5 us  [exchange(): pl.pallas_call(kernel, in_specs=[vmem] * count, out_specs=[vmem] * count,...]
    pallas_call x1, Pallas kernels: 72.1 us -> 64.1 us  [last_sums(): pl.pallas_call(kernel, in_specs=[vmem] * (len(grads) + 8), out_specs=[vme...]
    unnamed x76 -> x70, local copies, waits for them, and re-layouts: 22.8 us -> 23.9 us
  transfers between devices with their start and end apart: 9 -> 9, of which waited for: 5 -> 5; matrix products, arithmetic and copies ran while one was open for 5% -> 5% of each run, Pallas kernels for 34% -> 40%
where the time goes in v1:
time: 481 us; the launch traced here: 473 us
  Pallas kernels  336 us (70%)
  waiting for transfers between devices  45.6 us (9%)
  matrix products  37.6 us (8%)
  local copies, waits for them, and re-layouts  26.5 us (6%)
  other arithmetic  18.4 us (4%)
  starting transfers between devices  6.89 us (1%)
    pallas_call x1, Pallas kernels, sweep_backward(): pl.pallas_call(kernel, in_specs=in_specs, out_specs=[vmem] * 4, out_shape...  152 us
    pallas_call x3, Pallas kernels, exchange(): pl.pallas_call(kernel, in_specs=[vmem] * count, out_specs=[vmem] * count,...  65.5 us
    pallas_call x1, Pallas kernels, last_sums(): pl.pallas_call(kernel, in_specs=[vmem] * (len(grads) + 8), out_specs=[vme...  64.1 us
    pallas_call x2, Pallas kernels, sweep_forward(): pl.pallas_call(kernel, grid=(count // bq,), in_specs=in_specs, out_specs=...  48.1 us
    ppermute x3, waiting for transfers between devices, other_chip(): return lax.ppermute(block, 'tensor', [(i, i ^ 2) for i in range(4)])  40.2 us
    dot_general x15, matrix products, contract(): lax.dot_general(left, right, (((left_dim,), (right_dim,)), ((), ())), pre...  24.7 us
    unnamed x70, local copies, waits for them, and re-layouts  23.9 us
  transfers between devices with their start and end apart: 9, of which 5 were waited for; matrix products, arithmetic and copies ran while one was open for 5% of the time, Pallas kernels for 40%

profile of v1, /device:TPU:0, one launch (start us, length us, event | category | flops | bytes accessed | tf_op | source)
XLA Modules:
  0.0 473.2 jit_solution(16043289596898883976)
XLA Ops:
  0.7 2.2 copy.28
  2.9 2.0 copy.29
  4.9 1.3 pad_maximum_fusion.12
  6.2 5.8 %shard_map.220 = (bf16[1024,1024]{1,0:T(8,128)(2,1)}, f32[1024,1024]{1,0:T(8,128)}, f32[1024,1]{1,0:T(8,128)}) custom-call(s32[1]{0:T(128)} %bitcast.2.core_ref, bf16[1024,1024]{1,0:T(8,128)(2,1)} %tokens_ref.1, f32[1,1024]{1,0:T(1,128)} %bitcast.51, f32[1,1024]{1,0:T(1,128)} %bitcast.65), custom_call_target="tpu_custom_call" | custom-call | flops 10485760 | bytes 8388608 | tf_op jit(solution)/shard_map/pallas_call | solution.py:63
  12.0 2.6 fusion.17.refs_0_
  14.6 1.3 convolution_convert_fusion.6.refs_1_
  15.9 31.6 %shard_map.221 = (bf16[64,4096]{1,0:T(8,128)(2,1)S(1)}, bf16[4096,128]{1,0:T(8,128)(2,1)S(1)}) custom-call(bf16[256,1024]{1,0:T(8,128)(2,1)S(1)} %fusion.17.refs_0_, bf16[1024,512]{1,0:T(8,128)(2,1)S(1)} %convolution_convert_fusion.6.refs_1_), custom_call_target="tpu_custom_call" | custom-call | bytes 62914560 | tf_op jit(solution)/shard_map/pallas_call | solution.py:226
  48.3 1.5 collective-permute-start
  51.5 21.7 %shard_map.222 = (f32[1,4096]{1,0:T(1,128)S(1)}, f32[80,4096]{1,0:T(8,128)S(1)}) custom-call(s32[1]{0:T(128)} %bitcast.9.refs_0_, bf16[64,4096]{1,0:T(8,128)(2,1)S(1)} %copy-done.12, bf16[4096,128]{1,0:T(8,128)(2,1)S(1)} %get-tuple-element.42.refs_2_.refs_4_), custom_call_target="tpu_custom_call" | custom-call | flops 17179869184 | bytes 8388608 | tf_op jit(solution)/shard_map/pallas_call | solution.py:148
  73.4 26.4 %shard_map.223 = (f32[64,4096]{1,0:T(8,128)S(1)}, bf16[64,4096]{1,0:T(8,128)(2,1)S(1)}, f32[1,4096]{1,0:T(1,128)S(1)}) custom-call(s32[1]{0:T(128)} %bitcast.1.refs_0_, bf16[64,4096]{1,0:T(8,128)(2,1)S(1)} %copy-done.12, bf16[4096,128]{1,0:T(8,128)(2,1)} %collective-permute-done.refs_2_.refs_3_, f32[1,4096]{1,0:T(1,128)S(1)} %get-tuple-element.43.refs_3_, ...), custom_call_target="tpu_custom_call" | custom-call | flops 17179869184 | bytes 8388608 | tf_op jit(solution)/shard_map/pallas_call | solution.py:148
  99.8 20.2 %shard_map.224 = bf16[256,1024]{1,0:T(8,128)(2,1)S(1)} custom-call(bf16[64,4096]{1,0:T(8,128)(2,1)S(1)} %get-tuple-element.45.refs_0_), custom_call_target="tpu_custom_call" | custom-call | bytes 20971520 | tf_op jit(solution)/shard_map/pallas_call | solution.py:226
  120.6 2.6 collective-permute-done.1
  123.2 1.4 add_convert_fusion.4
  124.7 1.5 collective-permute-start.2
  126.2 24.0 %collective-permute-done.2 = bf16[512,1024]{1,0:T(8,128)(2,1)} collective-permute-done((bf16[512,1024]{1,0:T(8,128)(2,1)}, bf16[512,1024]{1,0:T(8,128)(2,1)}, u32[]{:S(2)}, u32[]{:S(2)}) %collective-permute-start.2) | collective-permute-done | bytes 1048608 | tf_op jit(solution)/shard_map/ppermute | solution.py:761
  150.2 2.9 fusion.38
  156.8 2.4 fusion.9
  159.2 6.7 %multiply_convert_fusion = (bf16[1024,1024]{1,0:T(8,128)(2,1)S(1)}, bf16[1024,1024]{1,0:T(8,128)(2,1)S(1)}) fusion(f32[1024,1024]{1,0:T(8,128)S(1)} %fusion.9, bf16[1024,1024]{1,0:T(8,128)(2,1)S(1)} %copy-done, bf16[512,1024]{1,0:T(8,128)(2,1)S(1)} %collective-permute-done.3, bf16[512,1024]{1,0:T(8,128)(2,1)S(1)} %add_convert_fusion.3), kind=kOutput, calls=%fused_computation.9 | convolution fusion | flops 2174746624 | bytes 12582912 | tf_op jit(solution)/shard_map/dot_general | solution.py:798
  165.8 1.3 convolution_convert_fusion.4
  167.2 2.6 collective-permute-done.4
  169.8 1.3 add_convert_fusion.2
  171.1 1.6 collective-permute-start.5
  172.7 3.7 convolution_convert_fusion.1.refs_6_
  176.5 3.7 convolution_convert_fusion.refs_7_
  180.2 16.2 %collective-permute-done.5 = bf16[512,1024]{1,0:T(8,128)(2,1)S(1)} collective-permute-done((bf16[512,1024]{1,0:T(8,128)(2,1)S(1)}, bf16[512,1024]{1,0:T(8,128)(2,1)S(1)}, u32[]{:S(2)}, u32[]{:S(2)}) %collective-permute-start.5) | collective-permute-done | bytes 1048608 | tf_op jit(solution)/shard_map/ppermute | solution.py:761
  197.5 1.3 convolution_convert_fusion.2
  198.8 2.3 multiply_convert_fusion.2
  201.7 2.2 add_convert_fusion.1
  203.9 1.5 collective-permute-start.8
  206.2 13.8 %shard_map.225.refs_1_ = bf16[64,4096]{1,0:T(8,128)(2,1)S(1)} custom-call(bf16[256,1024]{1,0:T(8,128)(2,1)S(1)} %fusion.18.refs_0_), custom_call_target="tpu_custom_call" | custom-call | bytes 20971520 | tf_op jit(solution)/shard_map/pallas_call | solution.py:226
  220.0 152.3 %shard_map.226 = (bf16[1024,512]{1,0:T(8,128)(2,1)S(1)}, bf16[256,1024]{1,0:T(8,128)(2,1)S(1)}, bf16[1024,1024]{1,0:T(8,128)(2,1)}, bf16[1024,1024]{1,0:T(8,128)(2,1)}) custom-call(bf16[64,4096]{1,0:T(8,128)(2,1)S(1)} %copy-done.13, bf16[64,4096]{1,0:T(8,128)(2,1)S(1)} %shard_map.225.refs_1_, f32[64,4096]{1,0:T(8,128)S(1)} %copy-done.15, ...), custom_call_target="tpu_custom_call" | custom-call | flops 85899345920 | bytes 20971520 | tf_op jit(solution)/shard_map/pallas_call | solution.py:502
  372.3 1.5 fusion.14.refs_0_
  373.9 2.5 convert_element_type.157
  376.4 2.5 convert_element_type.158
  381.2 1.3 convolution_convert_fusion.3.refs_1_
  382.5 1.6 convolution_convert_fusion.7.refs_2_
  384.5 2.4 copy-done.25
  387.0 2.3 multiply_reduce_fusion.1
  389.3 2.1 add_convert_fusion.refs_10_
  393.5 64.1 %shard_map.227 = (bf16[256,1024]{1,0:T(8,128)(2,1)S(1)}, bf16[1024,512]{1,0:T(8,128)(2,1)S(1)}, bf16[1024,256]{1,0:T(8,128)(2,1)S(1)}, bf16[1024,1024]{1,0:T(8,1...) custom-call(bf16[256,1024]{1,0:T(8,128)(2,1)S(1)} %copy-done.6, ...), custom_call_target="tpu_custom_call" | custom-call | bytes 157286400 | tf_op jit(solution)/shard_map/pallas_call | solution.py:711
  457.6 1.3 copy-done.2
  460.5 1.0 convert_element_type.155
  461.6 1.1 convert_element_type.156
  463.2 1.2 fusion.39
  464.4 2.5 copy.34
  466.9 1.3 copy.33
  468.2 3.2 copy.41
  471.4 1.3 copy.42
  (93 shorter events, 15.8 us)
Async XLA Ops:
  0.6 158.5 %copy-start = (bf16[1024,1024]{1,0:T(8,128)(2,1)S(1)}, bf16[1024,1024]{1,0:T(8,128)(2,1)}, u32[]{:S(2)}) copy-start(bf16[1024,1024]{1,0:T(8,128)(2,1)} %param.23) | copy-start | bytes 6291460
  6.2 8.4 %copy-start.17 = (bf16[1024,4,128]{0,2,1:T(8,128)(2,1)}, bf16[1024,4,128]{0,2,1:T(8,128)(2,1)S(1)}, u32[]{:S(2)}) copy-start(bf16[1024,4,128]{0,2,1:T(8,128)(2,1)S(1)} %pad_maximum_fusion.12) | copy-start | bytes 3145732
  12.0 2.6 copy-start.30
  47.5 0.8 copy-start.11
  48.3 25.0 %copy-start.9 = (bf16[4096,128]{1,0:T(8,128)(2,1)}, bf16[4096,128]{1,0:T(8,128)(2,1)S(1)}, u32[]{:S(2)}) copy-start(bf16[4096,128]{1,0:T(8,128)(2,1)S(1)} %get-tuple-element.42.refs_2_.refs_4_) | copy-start | bytes 3145732
  48.3 25.1 %collective-permute-start = (bf16[4096,128]{1,0:T(8,128)(2,1)S(1)}, bf16[4096,128]{1,0:T(8,128)(2,1)}, u32[]{:S(2)}, u32[]{:S(2)}) collective-permute-start(bf16[4096,128]{1,0:T(8,128)(2,1)S(1)} %get-tuple-element.42.refs_2_.refs_4_), channel_id=1, source_target_pairs={{0,4},{4,0},{8,12},{12,8},{16,20},{20,16},{24,28},{28,24},{1,5},{5... | collective-permute-start | bytes 3145736 | tf_op jit(solution)/shard_map/ppermute | solution.py:755
  50.5 1.0 copy-start.12
  73.4 46.6 %copy-start.23 = (bf16[256,1024]{1,0:T(8,128)(2,1)S(1)}, bf16[256,1024]{1,0:T(8,128)(2,1)}, u32[]{:S(2)}) copy-start(bf16[256,1024]{1,0:T(8,128)(2,1)} %param.20) | copy-start | bytes 1572868
  99.8 24.8 %copy-start.14 = (f32[64,4096]{1,0:T(8,128)}, f32[64,4096]{1,0:T(8,128)S(1)}, u32[]{:S(2)}) copy-start(f32[64,4096]{1,0:T(8,128)S(1)} %get-tuple-element.47.refs_2_) | copy-start | bytes 3145732
  120.5 2.7 collective-permute-start.1
  124.7 25.5 %collective-permute-start.2 = (bf16[512,1024]{1,0:T(8,128)(2,1)}, bf16[512,1024]{1,0:T(8,128)(2,1)}, u32[]{:S(2)}, u32[]{:S(2)}) collective-permute-start(bf16[512,1024]{1,0:T(8,128)(2,1)} %add_convert_fusion.4), channel_id=1, source_target_pairs={{0,2},{1,3},{2,0},{3,1},{4,6},{5,7},{6,4},{7,5},{8,10},{9,11},{10,... | collective-permute-start | bytes 3145736 | tf_op jit(solution)/shard_map/ppermute | solution.py:761
  153.0 0.7 copy-start.27
  153.0 0.7 copy-start.28
  153.4 1.6 copy-start.19
  154.1 5.0 %collective-permute-start.3 = (bf16[512,1024]{1,0:T(8,128)(2,1)S(1)}, bf16[512,1024]{1,0:T(8,128)(2,1)S(1)}, u32[]{:S(2)}, u32[]{:S(2)}) collective-permute-start(bf16[512,1024]{1,0:T(8,128)(2,1)S(1)} %add_convert_fusion.3), channel_id=1, source_target_pairs={{0,1},{1,0},{2,3},{3,2},{4,5},{5,4},{6,7},{7,6},{8,9},{9,8},{10,11... | collective-permute-start | bytes 3145736 | tf_op jit(solution)/shard_map/ppermute | solution.py:758
  155.2 1.6 copy-start.29
  167.1 2.7 collective-permute-start.4
  171.1 25.3 %collective-permute-start.5 = (bf16[512,1024]{1,0:T(8,128)(2,1)S(1)}, bf16[512,1024]{1,0:T(8,128)(2,1)S(1)}, u32[]{:S(2)}, u32[]{:S(2)}) collective-permute-start(bf16[512,1024]{1,0:T(8,128)(2,1)S(1)} %add_convert_fusion.2), channel_id=1, source_target_pairs={{0,2},{1,3},{2,0},{3,1},{4,6},{5,7},{6,4},{7,5},{8,10},{9,11},{10,... | collective-permute-start | bytes 3145736 | tf_op jit(solution)/shard_map/ppermute | solution.py:761
  198.7 3.0 collective-permute-start.7
  198.8 2.8 copy-start.26
  201.2 4.3 collective-permute-start.6
  201.7 3.8 copy-start.24
  203.9 16.1 %copy-start.10 = (bf16[4096,128]{1,0:T(8,128)(2,1)S(1)}, bf16[4096,128]{1,0:T(8,128)(2,1)}, u32[]{:S(2)}) copy-start(bf16[4096,128]{1,0:T(8,128)(2,1)} %copy-done.9) | copy-start | bytes 3145732
  203.9 16.1 %copy-start.13 = (bf16[64,4096]{1,0:T(8,128)(2,1)S(1)}, bf16[64,4096]{1,0:T(8,128)(2,1)}, u32[]{:S(2)}) copy-start(bf16[64,4096]{1,0:T(8,128)(2,1)} %copy-done.11) | copy-start | bytes 1572868
  203.9 16.1 %copy-start.15 = (f32[64,4096]{1,0:T(8,128)S(1)}, f32[64,4096]{1,0:T(8,128)}, u32[]{:S(2)}) copy-start(f32[64,4096]{1,0:T(8,128)} %copy-done.14) | copy-start | bytes 3145732
  203.9 178.5 %collective-permute-start.8 = (bf16[512,1024]{1,0:T(8,128)(2,1)}, bf16[512,1024]{1,0:T(8,128)(2,1)}, u32[]{:S(2)}, u32[]{:S(2)}) collective-permute-start(bf16[512,1024]{1,0:T(8,128)(2,1)} %add_convert_fusion.1), channel_id=1, source_target_pairs={{0,2},{1,3},{2,0},{3,1},{4,6},{5,7},{6,4},{7,5},{8,10},{9,11},{10,... | collective-permute-start | bytes 3145736 | tf_op jit(solution)/shard_map/ppermute | solution.py:761
  372.3 1.6 copy-start.21
  373.9 2.5 copy-start.20
  376.4 2.5 copy-start.18
  379.6 1.6 copy-start.31
  382.5 1.6 copy-start.22
  384.0 2.9 copy-start.25
  384.5 4.7 %copy-start.16 = (f32[512,1024]{1,0:T(8,128)}, f32[512,1024]{1,0:T(8,128)S(1)}, u32[]{:S(2)}) copy-start(f32[512,1024]{1,0:T(8,128)S(1)} %convolution_add_fusion.refs_4_) | copy-start | bytes 6291460
  389.3 2.1 copy-start.8
  391.4 1.0 copy-start.6
  392.5 1.0 copy-start.7
  457.6 1.3 copy-start.2
  458.9 1.0 copy-start.4
  459.9 2.8 copy-start.5
  468.2 3.2 copy-start.3
  468.2 4.6 copy-start.1
